TPU v7x, 768 devices: a whole 4x8x12 slice. The times are simulated.
768 devices in a mesh: seq: 96 (over x, z, core), head: 8 (over y).
Axes of the slice: x: 4, y: 8, z: 12, core: 2. Of those that a mesh axis runs over, the one named last changes fastest.
Arguments:
- query_rows: bfloat16 [24576, 4096], P('seq', 'head'), may hold values from -6 to 6
- key_rows: bfloat16 [24576, 4096], P('seq', 'head'), may hold values from -6 to 6
- value_rows: bfloat16 [24576, 4096], P('seq', 'head'), may hold values from -150 to 150
- log_decay: float32 [32, 24576], P('head', 'seq'), may hold values from -3 to 0
- out_grad: bfloat16 [24576, 4096], P('seq', 'head'), may hold values from -6 to 6
- norm_gain: float32 [4096], P('head'), may hold values from 0.1 to 1.9
- state_in: float32 [32, 128, 128], P('head'), may hold values from -96 to 96
- state_out_grad: float32 [32, 128, 128], P('head'), may hold values from -0.4375 to 0.4375
Outputs:
- query_grad: bfloat16 [24576, 4096], P('seq', 'head')
- key_grad: bfloat16 [24576, 4096], P('seq', 'head')
- value_grad: bfloat16 [24576, 4096], P('seq', 'head')
- state_in_grad: float32 [32, 128, 128], P('head')
All inputs are finite; a program needn't handle non-finite values.
Results may differ from a plain program's by a relative error of at most 0.0059.
Values sent between devices are 32-bit elements; how exact they have to be, the bound alone decides.
A program may use at most 128 MiB of HBM per device.

v0:
```python
import jax
import jax.numpy as jnp
from jax import lax
from jax.sharding import PartitionSpec as P

EPSILON = 1e-06


def prefix(value, axis, join, neutral, backward):
    count, mine = (lax.axis_size(axis), lax.axis_index(axis))
    pieces = jax.tree.map(lambda part: lax.all_gather(part, axis), value)
    if backward:
        pieces = jax.tree.map(lambda part: part[::-1], pieces)
        mine = count - 1 - mine
    total = jax.tree.map(
        lambda part, zero: jnp.full_like(part, 0) + jnp.asarray(zero, part.dtype), value, neutral
    )

    def step(position, total):
        longer = join(total, jax.tree.map(lambda part: part[position], pieces))
        return jax.tree.map(lambda new, old: jnp.where(position < mine, new, old), longer, total)

    return lax.fori_loop(0, count - 1, step, total)


def decay_tables(decay_rows):
    cum_log = jnp.cumsum(decay_rows, axis=1)
    block_log = cum_log[:, -1]
    length = decay_rows.shape[1]
    causal = jnp.arange(length)[:, None] >= jnp.arange(length)[None, :]
    spread = cum_log[:, :, None] - cum_log[:, None, :]
    decay_mat = jnp.where(causal[None], jnp.exp(jnp.minimum(spread, 0.0)), 0.0)
    return (cum_log, block_log, decay_mat)


def forward_combine(earlier_part, later_part):
    log_early, states_early = earlier_part
    log_late, states_late = later_part
    return (log_early + log_late, jnp.exp(log_late)[:, None, None] * states_early + states_late)


def reverse_combine(earlier_part, later_part):
    log_high, grads_high = earlier_part
    log_low, grads_low = later_part
    return (log_low + log_high, grads_low + jnp.exp(log_low)[:, None, None] * grads_high)


def head_major(rows, head_local, head_size):
    return rows.reshape(rows.shape[0], head_local, head_size).transpose(1, 0, 2)


def token_major(heads):
    return heads.astype(jnp.bfloat16).transpose(1, 0, 2).reshape(heads.shape[1], -1)


def on_device(
    query_rows, key_rows, value_rows, log_decay, out_grad, norm_gain, state_in, state_out_grad
):
    head_local = log_decay.shape[0]
    head_size = state_in.shape[1]
    feature_count = query_rows.shape[1] * lax.axis_size("head")
    query_heads = head_major(query_rows, head_local, head_size)
    key_heads = head_major(key_rows, head_local, head_size)
    value_heads = head_major(value_rows, head_local, head_size)
    upstream = head_major(out_grad, head_local, head_size)
    cum_log, block_log, decay_mat = decay_tables(log_decay)
    growth = jnp.exp(cum_log)[:, :, None]
    shrink = jnp.exp(block_log[:, None] - cum_log)[:, :, None]
    seq_index = lax.axis_index("seq")
    is_last = seq_index == lax.axis_size("seq") - 1
    key_decayed = (key_heads * shrink).astype(jnp.bfloat16)
    summary = jnp.einsum(
        "hsd,hse->hde", key_decayed, value_heads, preferred_element_type=jnp.float32
    )
    prefix_log, prefix_states = prefix(
        (block_log, summary),
        "seq",
        forward_combine,
        (jnp.zeros_like(block_log), jnp.zeros_like(summary)),
        False,
    )
    states_prev = prefix_states + jnp.exp(prefix_log)[:, None, None] * state_in
    states_bf = states_prev.astype(jnp.bfloat16)
    raw_scores = jnp.einsum(
        "htd,hsd->hts", query_heads, key_heads, preferred_element_type=jnp.float32
    )
    weights = (raw_scores * decay_mat).astype(jnp.bfloat16)
    attended = jnp.einsum("hts,hsd->htd", weights, value_heads, preferred_element_type=jnp.float32)
    attended = attended + growth * jnp.einsum(
        "htd,hde->hte", query_heads, states_bf, preferred_element_type=jnp.float32
    )
    gain_heads = norm_gain.reshape(head_local, 1, head_size)
    gained = gain_heads * upstream
    local_square = jnp.sum(attended * attended, axis=(0, 2))
    local_inner = jnp.sum(gained * attended, axis=(0, 2))
    total_square, total_inner = lax.psum((local_square, local_inner), "head")
    inv_rms = lax.rsqrt(total_square / feature_count + EPSILON)
    coefficient = total_inner * inv_rms**3 / feature_count
    attn_grad = (gained * inv_rms[None, :, None] - attended * coefficient[None, :, None]).astype(
        jnp.bfloat16
    )
    query_decayed = (query_heads * growth).astype(jnp.bfloat16)
    grad_summary = jnp.einsum(
        "htd,hte->hde", query_decayed, attn_grad, preferred_element_type=jnp.float32
    )
    suffix_log, suffix_states = prefix(
        (block_log, grad_summary),
        "seq",
        reverse_combine,
        (jnp.zeros_like(block_log), jnp.zeros_like(grad_summary)),
        True,
    )
    grads_next = suffix_states + jnp.exp(suffix_log)[:, None, None] * state_out_grad
    grads_bf = grads_next.astype(jnp.bfloat16)
    score_grad = (
        jnp.einsum("hte,hse->hts", attn_grad, value_heads, preferred_element_type=jnp.float32)
        * decay_mat
    ).astype(jnp.bfloat16)
    query_grad = jnp.einsum(
        "hts,hsd->htd", score_grad, key_heads, preferred_element_type=jnp.float32
    )
    query_grad = query_grad + growth * jnp.einsum(
        "hte,hde->htd", attn_grad, states_bf, preferred_element_type=jnp.float32
    )
    key_grad = jnp.einsum(
        "hts,htd->hsd", score_grad, query_heads, preferred_element_type=jnp.float32
    )
    key_grad = key_grad + shrink * jnp.einsum(
        "hde,hse->hsd", grads_bf, value_heads, preferred_element_type=jnp.float32
    )
    value_grad = jnp.einsum("hts,hte->hse", weights, attn_grad, preferred_element_type=jnp.float32)
    value_grad = value_grad + shrink * jnp.einsum(
        "hde,hsd->hse", grads_bf, key_heads, preferred_element_type=jnp.float32
    )
    own_term = jnp.exp(prefix_log)[:, None, None] * grad_summary
    own_term = own_term + jnp.where(
        is_last, jnp.exp(prefix_log + block_log)[:, None, None] * state_out_grad, 0.0
    )
    state_in_grad = lax.psum(own_term, "seq")
    return (token_major(query_grad), token_major(key_grad), token_major(value_grad), state_in_grad)


def solution(mesh):
    return jax.shard_map(
        on_device,
        mesh=mesh,
        in_specs=(
            P("seq", "head"),
            P("seq", "head"),
            P("seq", "head"),
            P("head", "seq"),
            P("seq", "head"),
            P("head"),
            P("head", None, None),
            P("head", None, None),
        ),
        out_specs=(P("seq", "head"), P("seq", "head"), P("seq", "head"), P("head", None, None)),
        check_vma=False,
    )
```

profile of v0, /device:TPU:1, one launch (start us, length us, event | category | flops | bytes accessed | tf_op | source)
XLA Modules:
  0.0 888.1 jit_solution(4935385326514838917)
XLA Ops:
  8.0 1.2 reduce-window.6
  9.8 2.2 fusion.18
  12.1 1.3 dynamic-slice
  14.1 198.0 %all-reduce = f32[384]{0:T(512)S(1)} all-reduce(f32[384]{0:T(512)S(1)} %bitcast_dynamic-update-slice_fusion), channel_id=2, replica_groups=mesh['seq'=96,'head'=8] {'seq'}, use_global_device_ids=true, to_apply=%add | all-reduce | flops 384 | bytes 3072
  212.2 1.1 copy.82
  213.3 1.1 copy.52
  214.9 1.3 fusion.20
  216.2 104.6 %while.32 = (s32[]{:T(128)}, f32[4]{0:T(128)S(1)}, f32[4,128,128]{2,1,0:T(8,128)S(1)}, s32[]{:T(128)}, f32[96,4]{1,0:T(8,128)S(1)}, /*index=5*/f32[96,4,128,128]{3,2,1,0:T(8,128)}, s32[]{:T(128)}, s32[]{:T(128)}) while((s32[]{:T(128)}, f32[4]{0:T(128)S(1)}, f32[4,128,128]{2,1,0:T(8,128)S(1)}, s32[]{:T(128)}, ...), condition=%wide.region_3.4_spmd.clone, body=%wide.region_2.3_spmd.clone.sunk | while | flops 262160 | bytes 786627 | solution.py:23
  221.7 1.1 fusion.59
  222.8 1.1 fusion.59
  223.9 1.1 fusion.59
  225.0 1.1 fusion.59
  226.1 1.1 fusion.59
  227.2 1.1 fusion.59
  228.3 1.1 fusion.59
  229.4 1.1 fusion.59
  230.6 1.1 fusion.59
  242.7 1.1 fusion.59
  243.8 1.1 fusion.59
  244.9 1.1 fusion.59
  246.0 1.1 fusion.59
  247.1 1.1 fusion.59
  248.2 1.1 fusion.59
  249.3 1.1 fusion.59
  250.4 1.1 fusion.59
  322.9 13.7 %all-reduce.1 = (f32[256]{0:T(256)S(1)}, f32[256]{0:T(256)S(1)}) all-reduce(f32[256]{0:T(256)S(1)} %get-tuple-element.283, f32[256]{0:T(256)S(1)} %get-tuple-element.282), channel_id=1, replica_groups=mesh['seq'=96,'head'=8] {'head'}, use_global_device_ids=true, to_apply=%region_7.8 | all-reduce | flops 512 | bytes 4096 | tf_op jit(solution)/shard_map/psum | solution.py:96
  338.5 1.4 fusion.3
  341.8 148.7 %all-gather.8.cloned.1.call-done = f32[384,128,128]{2,1,0:T(8,128)} async-done(((f32[4,128,128]{2,1,0:T(8,128)}), f32[384,128,128]{2,1,0:T(8,128)}) %all-gather.8.cloned.1.call-update) | async-done | bytes 25165840 | tf_op jit(solution)/shard_map/all_gather | solution.py:11
  490.5 17.3 %rev.7 = f32[96,4,128,128]{3,2,1,0:T(8,128)} reverse(f32[96,4,128,128]{3,2,1,0:T(8,128)} %bitcast.168), dimensions={0} | reverse | bytes 50331648 | tf_op jit(solution)/shard_map/rev | solution.py:13
  507.8 104.6 %while.33 = (s32[]{:T(128)}, f32[4]{0:T(128)S(1)}, f32[4,128,128]{2,1,0:T(8,128)S(1)}, s32[]{:T(128)}, f32[96,4]{1,0:T(8,128)S(1)}, /*index=5*/f32[96,4,128,128]{3,2,1,0:T(8,128)}, s32[]{:T(128)}, s32[]{:T(128)}) while((s32[]{:T(128)}, f32[4]{0:T(128)S(1)}, f32[4,128,128]{2,1,0:T(8,128)S(1)}, s32[]{:T(128)}, ...), condition=%wide.region_9.10_spmd.clone, body=%wide.region_8.9_spmd.clone.sunk | while | flops 262160 | bytes 786627 | solution.py:23
  615.6 264.3 %all-reduce.4.cloned.1.call-done = f32[4,128,128]{2,1,0:T(8,128)} async-done(((f32[4,128,128]{2,1,0:T(8,128)}), f32[4,128,128]{2,1,0:T(8,128)}) %all-reduce.4.cloned.1.call-update) | async-done | bytes 262160 | tf_op jit(solution)/shard_map/psum | solution.py:139
  879.9 1.7 copy.151
  (416 shorter events, 197.1 us)
Async XLA Ops:
  7.2 2.6 copy-start
  7.2 209.0 %all-gather.6.cloned.1.call-start = ((), (), s32[]{:S(2)}) async-start(), calls=%async_computation.1 | async-start | bytes 25427968 | tf_op jit(solution)/shard_map/all_gather | solution.py:11
  12.0 478.5 %all-gather.8.cloned.1.call-start = ((), (), s32[]{:S(2)}) async-start(), calls=%async_computation.2 | async-start | bytes 25427968 | tf_op jit(solution)/shard_map/all_gather | solution.py:11
  338.5 541.4 %all-reduce.4.cloned.1.call-start = ((), (), s32[]{:S(2)}) async-start(), calls=%async_computation | async-start | bytes 524288 | tf_op jit(solution)/shard_map/psum | solution.py:139
  490.5 122.0 %copy-start.1 = (f32[4,128,128]{2,1,0:T(8,128)S(1)}, f32[4,128,128]{2,1,0:T(8,128)}, u32[]{:S(2)}) copy-start(f32[4,128,128]{2,1,0:T(8,128)} %fusion.19) | copy-start | bytes 786436
  490.5 122.0 %copy-start.3 = (f32[4,128,128]{2,1,0:T(8,128)S(1)}, f32[4,128,128]{2,1,0:T(8,128)}, u32[]{:S(2)}) copy-start(f32[4,128,128]{2,1,0:T(8,128)} %param.19) | copy-start | bytes 786436
  490.5 124.0 %copy-start.2 = (bf16[256,512]{1,0:T(8,128)(2,1)S(1)}, bf16[256,512]{1,0:T(8,128)(2,1)}, u32[]{:S(2)}) copy-start(bf16[256,512]{1,0:T(8,128)(2,1)} %param.14) | copy-start | bytes 786436
Sparse Core Ops, SparseCore 0:
  12.3 163.7 all-gather.5
  338.6 151.8 all-gather.7
  614.6 265.2 all-reduce.3
where the time goes:
time: 895 us; the launch traced here: 888 us
  waiting for transfers between devices  413 us (46%)
  blocking collectives  212 us (24%)
  other arithmetic  208 us (23%)
  local copies, waits for them, and re-layouts  26.4 us (3%)
  between operations  14.7 us (2%)
    psum x1, waiting for transfers between devices, on_device(): state_in_grad = lax.psum(own_term, 'seq')  264 us
    select_n x190, other arithmetic, step(): jnp.where(position < mine, new, old)  201 us
    unnamed x1, blocking collectives  198 us
    all_gather x2, waiting for transfers between devices, prefix(): pieces = jax.tree.map(lambda part: lax.all_gather(part, axis), value)  149 us
  transfers between devices with their start and end apart: 3, of which 2 were waited for; matrix products, arithmetic and copies ran while one was open for 1% of the time, Pallas kernels for 0%

commit v1 on v0

v1 whole, which is shorter than its diff:
```python
import jax
import jax.numpy as jnp
from jax import lax
from jax.experimental import pallas as pl
from jax.experimental.pallas import tpu as pltpu
from jax.sharding import PartitionSpec as P

EPSILON = 1e-06
MESH = pl.DeviceIdType.MESH
F32 = jnp.float32
BF16 = jnp.bfloat16

NX, NZ, NY = 4, 12, 8
CHIPS = NX * NZ
HL, TOK, DH = 4, 256, 128
TILES = 32
OWN_Z = 8


def far_first(step, count):
    return count // 2 + ((step + 1) // 2) * (1 - 2 * (step % 2))


def dot(a, b, dims):
    return lax.dot_general(a, b, (dims, ((), ())), preferred_element_type=F32)


NN = ((1,), (0,))
NT = ((1,), (1,))
TN = ((0,), (0,))


def kernel(
    q_hbm, k_hbm, v_hbm, ld_hbm, og_hbm, gain_hbm, sin_hbm, sout_hbm,
    qg_out, kg_out, vg_out, sg_out,
    q, k, v, og, gain, ld, tile_in, tile_out,
    cum_pad, cum_col, bl_mine, bl_other, dec_src, dec_all,
    sum_send, sum_recv, rows_pad, cols_pad,
    summ, summ_recv, t_src, t_all, p_src, p_ret, p_fwd, p_other,
    gsum, gsum_recv, u_src, u_all, h_src, h_ret, h_fwd, h_other, g_src, g_all,
    states_bf, grads_bf, dmat, wts, growth, shrink, attended, gained, qdec, agrad,
    kpart, vpart, qg, kg, vg,
    in_sem, x_send, x_recv, a_send, a_recv, out_sem,
):
    s = lax.axis_index("seq")
    y = lax.axis_index("head")
    c = s % 2
    p = s // 2
    x = p // NZ
    z = p % NZ
    is_owner = z % 3 != 2
    zi = (z // 3) * 2 + jnp.minimum(z % 3, 1)
    my_tile = x * OWN_Z + zi
    partner = (s + 1 - 2 * c, y)
    mine, theirs = 2 * c, 2 - 2 * c

    loads = {}

    def load(name, slot, src, dst):
        copy = pltpu.make_async_copy(src, dst, in_sem.at[slot])
        copy.start()
        loads.setdefault(name, []).append(copy)

    def arrived(name):
        for copy in loads[name]:
            copy.wait()

    load("ld", 0, ld_hbm, ld)
    for index, (name, src, dst) in enumerate((("k", k_hbm, k), ("v", v_hbm, v), ("q", q_hbm, q), ("og", og_hbm, og))):
        for h in range(HL):
            load(name, 1 + index * HL + h, src.at[:, pl.ds(h * DH, DH)], dst.at[h])
    load("gain", 17, gain_hbm, gain)
    load("tile", 18, sin_hbm.at[c * TILES + my_tile], tile_in)
    load("tile", 19, sout_hbm.at[c * TILES + my_tile], tile_out)

    def chip_at(step):
        dx = far_first(step % NX, NX)
        dz = far_first(step // NX, NZ)
        return ((x + dx) % NX) * NZ + (z + dz) % NZ

    barrier = pltpu.get_barrier_semaphore()

    def greet_chip(step, carry):
        pl.semaphore_signal(barrier, inc=1, device_id=(chip_at(step) * 2 + c, y), device_id_type=MESH)
        return carry

    lax.fori_loop(0, CHIPS - 1, greet_chip, 0)

    def greet_head(step, carry):
        pl.semaphore_signal(barrier, inc=1, device_id=(s, (y + 1 + step) % NY), device_id_type=MESH)
        return carry

    lax.fori_loop(0, NY - 1, greet_head, 0)
    pl.semaphore_signal(barrier, inc=1, device_id=partner, device_id_type=MESH)

    cum_pad[...] = jnp.zeros_like(cum_pad)
    arrived("ld")
    cum_pad[0:HL, :] = ld[...]
    cum = cum_pad[0:8, :]
    lane = lax.broadcasted_iota(jnp.int32, (8, TOK), 1)
    for shift in (1, 2, 4, 8, 16, 32, 64, 128):
        cum = cum + jnp.where(lane >= shift, pltpu.roll(cum, shift, 1), 0.0)
    cum_pad[0:8, :] = cum
    cum_col[...] = cum_pad[...].T
    bl = jnp.broadcast_to(cum[:, TOK - 1 : TOK], (8, DH))
    bl_mine[...] = bl

    pl.semaphore_wait(barrier, CHIPS - 1 + NY)

    def swap(slot, src, dst):
        copy = pltpu.make_async_remote_copy(
            src_ref=src, dst_ref=dst, send_sem=x_send.at[slot], recv_sem=x_recv.at[slot],
            device_id=partner, device_id_type=MESH,
        )
        copy.start()
        return copy

    swap_bl = swap(0, bl_mine, bl_other)

    arrived("k")
    arrived("v")
    for h in range(HL):
        fade = jnp.exp(cum_col[TOK - 1 : TOK, h : h + 1] - cum_col[:, h : h + 1])
        shrink[h] = jnp.broadcast_to(fade, (TOK, DH))
        key_decayed = (k[h].astype(F32) * shrink[h]).astype(BF16)
        summ[h] = dot(key_decayed, v[h], TN)
    swap_summ = swap(1, summ.at[pl.ds(theirs, 2)], summ_recv)

    def to_owners(src_of, dst, slot, keep):
        def send(step):
            xt = (x + far_first(step % NX, NX)) % NX
            zt = (zi + far_first(step // NX, OWN_Z)) % OWN_Z
            tile = xt * OWN_Z + zt
            chip = xt * NZ + (zt // 2) * 3 + zt % 2
            pltpu.make_async_remote_copy(
                src_ref=src_of(tile), dst_ref=dst.at[p], send_sem=a_send.at[slot], recv_sem=a_recv.at[slot],
                device_id=(chip * 2 + c, y), device_id_type=MESH,
            ).start()

        def body(step, carry):
            send(step)
            return carry

        lax.fori_loop(0, TILES - 1, body, 0)

        @pl.when(jnp.logical_not(is_owner))
        def _():
            send(TILES - 1)

        @pl.when(is_owner)
        def _():
            dst[p] = keep()

    def from_owner(src_of, dst, slot):
        def body(step, carry):
            chip = chip_at(step)
            pltpu.make_async_remote_copy(
                src_ref=src_of(chip), dst_ref=dst.at[c, my_tile], send_sem=a_send.at[slot], recv_sem=a_recv.at[slot],
                device_id=(chip * 2 + c, y), device_id_type=MESH,
            ).start()
            return carry

        lax.fori_loop(0, CHIPS - 1, body, 0)

    def drain(sem, ref, count):
        window = ref.at[pl.ds(0, count)]
        pltpu.make_async_copy(window, window, sem).wait()

    def drain_tiles(sem, ref):
        @pl.when(is_owner)
        def _():
            drain(sem, ref, TILES - 1)

        @pl.when(jnp.logical_not(is_owner))
        def _():
            drain(sem, ref, TILES)

    swap_bl.wait_recv()
    e_mine = jnp.exp(bl_mine[...])
    e_other = jnp.exp(bl_other[...])
    e_chip = jnp.exp(bl_mine[...] + bl_other[...])
    for h in range(HL):
        dec_src[h] = jnp.broadcast_to(e_chip[h : h + 1, :], (8, DH))
    to_owners(
        lambda tile: dec_src.at[mine + tile // 16], dec_all, 0, lambda: dec_src[mine + my_tile // 16]
    )

    first = c == 0

    def pick_rows(value):
        return [jnp.where(first, value[i : i + 1, :], value[2 + i : 3 + i, :]) for i in range(2)]

    e_first = jnp.where(first, e_mine, e_other)
    e_second = jnp.where(first, e_other, e_mine)
    e_first_rows, e_second_rows = pick_rows(e_first), pick_rows(e_second)

    swap_summ.wait_recv()
    for i in range(2):
        own, other = summ[mine + i], summ_recv[i]
        early = jnp.where(first, own, other)
        late = jnp.where(first, other, own)
        t_src[16 * i : 16 * i + 16] = (e_second_rows[i] * early + late).reshape(16, 8, DH)
    to_owners(lambda tile: t_src.at[tile], t_all, 1, lambda: t_src[my_tile])

    arrived("q")
    row_id = lax.broadcasted_iota(jnp.int32, (TOK, TOK), 0)
    col_id = lax.broadcasted_iota(jnp.int32, (TOK, TOK), 1)
    for h in range(HL):
        col = cum_col[:, h : h + 1]
        spread = col - cum_pad[h : h + 1, :]
        decay = jnp.where(row_id >= col_id, jnp.exp(jnp.minimum(spread, 0.0)), 0.0)
        dmat[h] = decay
        weights = (dot(q[h], k[h], NT) * decay).astype(BF16)
        wts[h] = weights
        attended[h] = dot(weights, v[h], NN)
        growth[h] = jnp.broadcast_to(jnp.exp(col), (TOK, DH))
        qdec[h] = (q[h].astype(F32) * growth[h]).astype(BF16)

    arrived("tile")

    @pl.when(is_owner)
    def _():
        drain(a_recv.at[0], dec_all, CHIPS - 1)
        drain(a_recv.at[1], t_all, CHIPS - 1)

        def body(chip, state):
            p_src[chip] = state
            return dec_all[chip] * state + t_all[chip]

        lax.fori_loop(0, CHIPS, body, tile_in[...], unroll=4)
        from_owner(lambda chip: p_src.at[chip], p_ret, 2)
        p_ret[c, my_tile] = p_src[p]

    arrived("og")
    arrived("gain")
    for h in range(HL):
        gained[h] = gain[:, h * DH : (h + 1) * DH] * og[h].astype(F32)

    drain_tiles(a_recv.at[2], p_ret.at[c])
    for i in range(2):
        chip_state = p_ret[c, 16 * i : 16 * i + 16].reshape(DH, DH)
        after = e_first_rows[i] * chip_state + jnp.where(first, summ[mine + i], summ_recv[i])
        p_fwd[i] = jnp.where(first, after, chip_state)
        states_bf[mine + i] = jnp.where(first, chip_state, after).astype(BF16)
    swap_state = swap(2, p_fwd, p_other)

    def attend(h, square, inner):
        state_part = dot(q[h], states_bf[h], NN)
        out = attended[h] + growth[h] * state_part
        attended[h] = out
        return square + out * out, inner + gained[h] * out

    square = jnp.zeros((TOK, DH), F32)
    inner = jnp.zeros((TOK, DH), F32)
    for i in range(2):
        square, inner = attend(mine + i, square, inner)
    swap_state.wait_recv()
    for i in range(2):
        states_bf[theirs + i] = p_other[i].astype(BF16)
    for i in range(2):
        square, inner = attend(theirs + i, square, inner)

    sum_send[0:1, :] = jnp.sum(square.T, axis=0, keepdims=True)
    sum_send[1:2, :] = jnp.sum(inner.T, axis=0, keepdims=True)

    def send_sums(step, carry):
        pltpu.make_async_remote_copy(
            src_ref=sum_send, dst_ref=sum_recv.at[y], send_sem=a_send.at[3], recv_sem=a_recv.at[3],
            device_id=(s, (y + far_first(step, NY)) % NY), device_id_type=MESH,
        ).start()
        return carry

    lax.fori_loop(0, NY - 1, send_sums, 0)
    sum_recv[y] = sum_send[...]
    rows_pad[...] = jnp.zeros_like(rows_pad)
    drain(a_recv.at[3], sum_recv, NY - 1)
    total = sum_recv[0]
    for i in range(1, NY):
        total = total + sum_recv[i]
    features = HL * DH * NY
    inv_rms = lax.rsqrt(total[0:1, :] / features + EPSILON)
    rows_pad[0:1, :] = inv_rms
    rows_pad[1:2, :] = total[1:2, :] * (inv_rms * inv_rms * inv_rms) / features
    cols_pad[...] = rows_pad[...].T
    inv_col = cols_pad[:, 0:1]
    coef_col = cols_pad[:, 1:2]

    for h in range(HL):
        grad = (gained[h] * inv_col - attended[h] * coef_col).astype(BF16)
        agrad[h] = grad
        gsum[h] = dot(qdec[h], grad, TN)
    swap_grad = swap(3, gsum.at[pl.ds(theirs, 2)], gsum_recv)

    def score_part(h):
        score = (dot(agrad[h], v[h], NT) * dmat[h]).astype(BF16)
        query_grad = dot(score, k[h], NN) + growth[h] * dot(agrad[h], states_bf[h], NT)
        qg[h] = query_grad.astype(BF16)
        kpart[h] = dot(score, q[h], TN)
        vpart[h] = dot(wts[h], agrad[h], TN)

    swap_grad.wait_recv()
    for i in range(2):
        own, other = gsum[mine + i], gsum_recv[i]
        early = jnp.where(first, own, other)
        late = jnp.where(first, other, own)
        u_src[16 * i : 16 * i + 16] = (e_first_rows[i] * late + early).reshape(16, 8, DH)
    to_owners(lambda tile: u_src.at[tile], u_all, 4, lambda: u_src[my_tile])

    stores = []

    def store(slot, src, dst):
        copy = pltpu.make_async_copy(src, dst, out_sem.at[slot])
        copy.start()
        stores.append(copy)

    for h in range(HL):
        score_part(h)
        store(h, qg.at[h], qg_out.at[:, pl.ds(h * DH, DH)])

    @pl.when(is_owner)
    def _():
        drain(a_recv.at[4], u_all, CHIPS - 1)

        def body(step, grad):
            chip = CHIPS - 1 - step
            h_src[chip] = grad
            return dec_all[chip] * grad + u_all[chip]

        g_src[...] = lax.fori_loop(0, CHIPS, body, tile_out[...], unroll=4)
        from_owner(lambda chip: h_src.at[chip], h_ret, 5)
        h_ret[c, my_tile] = h_src[p]
        from_owner(lambda chip: g_src, g_all, 6)
        g_all[c, my_tile] = g_src[...]

    drain_tiles(a_recv.at[5], h_ret.at[c])
    for i in range(2):
        chip_grad = h_ret[c, 16 * i : 16 * i + 16].reshape(DH, DH)
        before = e_second_rows[i] * chip_grad + jnp.where(first, gsum_recv[i], gsum[mine + i])
        h_fwd[i] = jnp.where(first, chip_grad, before)
        grads_bf[mine + i] = jnp.where(first, before, chip_grad).astype(BF16)
    swap_back = swap(4, h_fwd, h_other)

    def finish(h):
        key_grad = kpart[h] + shrink[h] * dot(v[h], grads_bf[h], NT)
        kg[h] = key_grad.astype(BF16)
        value_grad = vpart[h] + shrink[h] * dot(k[h], grads_bf[h], NN)
        vg[h] = value_grad.astype(BF16)

    for i in range(2):
        finish(mine + i)
    swap_back.wait_recv()
    for i in range(2):
        grads_bf[theirs + i] = h_other[i].astype(BF16)
    for i in range(2):
        finish(theirs + i)
    for h in range(HL):
        store(HL + h, kg.at[h], kg_out.at[:, pl.ds(h * DH, DH)])
        store(2 * HL + h, vg.at[h], vg_out.at[:, pl.ds(h * DH, DH)])

    drain_tiles(a_recv.at[6], g_all.at[c])
    swap_slab = swap(5, g_all.at[c], g_all.at[c])
    store(3 * HL, g_all.at[c], sg_out.at[c])
    swap_slab.wait_recv()
    store(3 * HL + 1, g_all.at[1 - c], sg_out.at[1 - c])

    for copy in (swap_bl, swap_summ, swap_state, swap_grad, swap_back, swap_slab):
        copy.wait_send()
    for slot, ref in ((0, t_src), (1, t_src), (4, u_src)):
        drain_tiles(a_send.at[slot], ref)
    drain(a_send.at[3], sum_recv, NY - 1)

    @pl.when(is_owner)
    def _():
        for slot in (2, 5, 6):
            drain(a_send.at[slot], p_src, CHIPS - 1)

    for copy in stores:
        copy.wait()


def on_device(query_rows, key_rows, value_rows, log_decay, out_grad, norm_gain, state_in, state_out_grad):
    any_space = pl.BlockSpec(memory_space=pl.ANY)

    def vm(*shape, dtype=F32):
        return pltpu.VMEM(shape, dtype)

    tiles = vm(TILES, 8, DH)
    landing = vm(CHIPS, 8, DH)
    halves = vm(2, TILES, 8, DH)
    pair = vm(2, DH, DH)
    heads = vm(HL, TOK, DH)
    heads_bf = vm(HL, TOK, DH, dtype=BF16)
    state = vm(HL, DH, DH)
    state_bf = vm(HL, DH, DH, dtype=BF16)
    dma = pltpu.SemaphoreType.DMA
    rows = jax.ShapeDtypeStruct(query_rows.shape, BF16)
    slab = jax.ShapeDtypeStruct((2, TILES, 8, DH), F32)
    qg, kg, vg, sg = pl.pallas_call(
        kernel,
        out_shape=(rows, rows, rows, slab),
        in_specs=[any_space] * 8,
        out_specs=(any_space,) * 4,
        scratch_shapes=[
            heads_bf, heads_bf, heads_bf, heads_bf, vm(1, HL * DH), vm(HL, TOK), vm(8, DH), vm(8, DH),
            vm(DH, TOK), vm(TOK, DH), vm(8, DH), vm(8, DH), vm(HL, 8, DH), landing,
            vm(2, TOK), vm(NY, 2, TOK), vm(DH, TOK), vm(TOK, DH),
            state, pair, tiles, landing, landing, halves, pair, pair,
            state, pair, tiles, landing, landing, halves, pair, pair, vm(8, DH), halves,
            state_bf, state_bf, vm(HL, TOK, TOK), vm(HL, TOK, TOK, dtype=BF16), heads, heads, heads, heads, heads_bf, heads_bf,
            heads, heads, heads_bf, heads_bf, heads_bf,
            dma((20,)), dma((6,)), dma((6,)), dma((7,)), dma((7,)), dma((3 * HL + 2,)),
        ],
        compiler_params=pltpu.CompilerParams(
            collective_id=0, has_side_effects=True, vmem_limit_bytes=48 * 1024 * 1024
        ),
    )(
        query_rows, key_rows, value_rows, log_decay, out_grad, norm_gain.reshape(1, HL * DH),
        state_in.reshape(2 * TILES, 8, DH), state_out_grad.reshape(2 * TILES, 8, DH),
    )
    return qg, kg, vg, sg.reshape(HL, DH, DH)


def solution(mesh):
    wide = P("seq", "head")
    state = P("head", None, None)
    return jax.shard_map(
        on_device,
        mesh=mesh,
        in_specs=(wide, wide, wide, P("head", "seq"), wide, P("head"), state, state),
        out_specs=(wide, wide, wide, state),
        check_vma=False,
    )
```

time: 895 us -> 88.3 us (0.10)
  waiting for transfers between devices: 413 us -> 0 us
  blocking collectives: 212 us -> 0 us
  other arithmetic: 208 us -> 0 us
  Pallas kernels: 0 us -> 77.4 us
  local copies, waits for them, and re-layouts: 26.4 us -> 9.87 us
  between operations: 14.7 us -> 0.66 us
    psum x1 -> x0, waiting for transfers between devices: 264 us -> none  [on_device(): state_in_grad = lax.psum(own_term, 'seq')]
    select_n x190 -> x0, other arithmetic: 201 us -> none  [step(): jnp.where(position < mine, new, old)]
    unnamed x1 -> x0, blocking collectives: 198 us -> none
    all_gather x2 -> x0, waiting for transfers between devices: 149 us -> none  [prefix(): pieces = jax.tree.map(lambda part: lax.all_gather(part, axis), value)]
    pallas_call x0 -> x1, Pallas kernels: none -> 77.4 us  [on_device(): pl.pallas_call(kernel, out_shape=(rows, rows, rows, slab), in_specs=[any_...]
    rev x2 -> x0, local copies, waits for them, and re-layouts: 17.4 us -> none  [prefix(): pieces = jax.tree.map(lambda part: part[::-1], pieces)]
    psum x1 -> x0, blocking collectives: 13.7 us -> none  [on_device(): total_square, total_inner = lax.psum((local_square, local_inner), 'head')]
  transfers between devices with their start and end apart: 3 -> 0, of which waited for: 2 -> 0; matrix products, arithmetic and copies ran while one was open for 1% -> 0% of each run, Pallas kernels for 0% -> 0%
where the time goes in v1:
time: 88.3 us; the launch traced here: 88 us
  Pallas kernels  77.4 us (88%)
  local copies, waits for them, and re-layouts  9.87 us (11%)
    pallas_call x1, Pallas kernels, on_device(): pl.pallas_call(kernel, out_shape=(rows, rows, rows, slab), in_specs=[any_...  77.4 us
    unnamed x20, local copies, waits for them, and re-layouts  9.87 us

profile of v1, /device:TPU:1, one launch (start us, length us, event | category | flops | bytes accessed | tf_op | source)
XLA Modules:
  0.0 88.0 jit_solution(18168256991207850676)
XLA Ops:
  0.6 0.0 copy-start.6
  0.6 0.7 copy-done.6
  1.3 0.0 copy-start
  1.3 0.9 %copy-done = bf16[256,512]{1,0:T(8,128)(2,1)S(1)} copy-done((bf16[256,512]{1,0:T(8,128)(2,1)S(1)}, bf16[256,512]{1,0:T(8,128)(2,1)}, u32[]{:S(2)}) %copy-start) | copy-done | bytes 262168
  2.3 0.0 copy-start.1
  2.3 0.9 %copy-done.1 = bf16[256,512]{1,0:T(8,128)(2,1)S(1)} copy-done((bf16[256,512]{1,0:T(8,128)(2,1)S(1)}, bf16[256,512]{1,0:T(8,128)(2,1)}, u32[]{:S(2)}) %copy-start.1) | copy-done | bytes 262168
  3.2 0.0 copy-start.2
  3.2 0.9 %copy-done.2 = bf16[256,512]{1,0:T(8,128)(2,1)S(1)} copy-done((bf16[256,512]{1,0:T(8,128)(2,1)S(1)}, bf16[256,512]{1,0:T(8,128)(2,1)}, u32[]{:S(2)}) %copy-start.2) | copy-done | bytes 262168
  4.2 0.0 copy-start.3
  4.2 0.9 %copy-done.3 = bf16[256,512]{1,0:T(8,128)(2,1)S(1)} copy-done((bf16[256,512]{1,0:T(8,128)(2,1)S(1)}, bf16[256,512]{1,0:T(8,128)(2,1)}, u32[]{:S(2)}) %copy-start.3) | copy-done | bytes 262168
  5.1 0.0 copy-start.4
  5.1 0.9 %copy-done.4 = f32[4,128,128]{2,1,0:T(8,128)S(1)} copy-done((f32[4,128,128]{2,1,0:T(8,128)S(1)}, f32[4,128,128]{2,1,0:T(8,128)}, u32[]{:S(2)}) %copy-start.4) | copy-done | bytes 262168
  6.1 0.0 copy-start.5
  6.1 0.9 %copy-done.5 = f32[4,128,128]{2,1,0:T(8,128)S(1)} copy-done((f32[4,128,128]{2,1,0:T(8,128)S(1)}, f32[4,128,128]{2,1,0:T(8,128)}, u32[]{:S(2)}) %copy-start.5) | copy-done | bytes 262168
  7.0 0.0 copy-start.7
  7.0 0.7 copy-done.7
  7.7 77.4 %shard_map.111 = (bf16[256,512]{1,0:T(8,128)(2,1)S(1)}, bf16[256,512]{1,0:T(8,128)(2,1)S(1)}, bf16[256,512]{1,0:T(8,128)(2,1)S(1)}, f32[2,32,8,128]{3,2,1,0:T(8,128)S(1)}) custom-call(bf16[256,512]{1,0:T(8,128)(2,1)S(1)} %copy-done, bf16[256,512]{1,0:T(8,128)(2,1)S(1)} %copy-done.1, bf16[256,512]{1,0:T(8,128)(2,1)S(1)} %copy-done.2, f32[4,256]{1,0:T(4,128)S(1)} %copy-done.6, ...), custom_call_target="tpu_custom_call" | custom-call | tf_op jit(solution)/shard_map/pallas_call | solution.py:398
  85.1 0.7 copy.16
  85.9 0.7 copy.17
  86.6 0.7 copy.18
  87.3 0.7 copy.19
Async XLA Ops:
  0.6 0.7 copy-start.6
  1.3 0.9 %copy-start = (bf16[256,512]{1,0:T(8,128)(2,1)S(1)}, bf16[256,512]{1,0:T(8,128)(2,1)}, u32[]{:S(2)}) copy-start(bf16[256,512]{1,0:T(8,128)(2,1)} %q_hbm.1) | copy-start | bytes 786436
  2.3 0.9 %copy-start.1 = (bf16[256,512]{1,0:T(8,128)(2,1)S(1)}, bf16[256,512]{1,0:T(8,128)(2,1)}, u32[]{:S(2)}) copy-start(bf16[256,512]{1,0:T(8,128)(2,1)} %k_hbm.1) | copy-start | bytes 786436
  3.2 0.9 %copy-start.2 = (bf16[256,512]{1,0:T(8,128)(2,1)S(1)}, bf16[256,512]{1,0:T(8,128)(2,1)}, u32[]{:S(2)}) copy-start(bf16[256,512]{1,0:T(8,128)(2,1)} %v_hbm.1) | copy-start | bytes 786436
  4.2 0.9 %copy-start.3 = (bf16[256,512]{1,0:T(8,128)(2,1)S(1)}, bf16[256,512]{1,0:T(8,128)(2,1)}, u32[]{:S(2)}) copy-start(bf16[256,512]{1,0:T(8,128)(2,1)} %og_hbm.1) | copy-start | bytes 786436
  5.1 0.9 %copy-start.4 = (f32[4,128,128]{2,1,0:T(8,128)S(1)}, f32[4,128,128]{2,1,0:T(8,128)}, u32[]{:S(2)}) copy-start(f32[4,128,128]{2,1,0:T(8,128)} %param.14) | copy-start | bytes 786436
  6.1 0.9 %copy-start.5 = (f32[4,128,128]{2,1,0:T(8,128)S(1)}, f32[4,128,128]{2,1,0:T(8,128)}, u32[]{:S(2)}) copy-start(f32[4,128,128]{2,1,0:T(8,128)} %param.15) | copy-start | bytes 786436
  7.0 0.7 copy-start.7

commit v2 on v1

v2 whole, which is shorter than its diff:
```python
import jax
import jax.numpy as jnp
from jax import lax
from jax.experimental import pallas as pl
from jax.experimental.pallas import tpu as pltpu
from jax.sharding import PartitionSpec as P

EPSILON = 1e-06
MESH = pl.DeviceIdType.MESH
F32 = jnp.float32
BF16 = jnp.bfloat16

NX, NZ, NY = 4, 12, 8
CHIPS = NX * NZ
HL, TOK, DH = 4, 256, 128
TILES = 32
OWN_Z = 8
X_STEPS = (2, 1, 3, 0)
Y_STEPS = (4, 3, 5, 2, 6, 1, 7)


def far_first(step, count):
    return count // 2 + ((step + 1) >> 1) * (1 - 2 * (step & 1))


def dot(a, b, dims):
    return lax.dot_general(a, b, (dims, ((), ())), preferred_element_type=F32)


NN = ((1,), (0,))
NT = ((1,), (1,))
TN = ((0,), (0,))


def at_least(value, bounds):
    return sum((value >= bound).astype(jnp.int32) for bound in bounds)


def kernel(
    q_hbm, k_hbm, v_hbm, ld_hbm, og_hbm, gain_hbm, sin_hbm, sout_hbm,
    qg, kg, vg, sg,
    q, k, v, og, gain, ld, tile_in, tile_out,
    cum_pad, cum_col, bl_mine, bl_other, dec_src, dec_all,
    sum_send, sum_recv, rows_pad, cols_pad,
    summ, summ_recv, t_src, t_all, p_src, p_ret, p_fwd, p_other,
    gsum, gsum_recv, u_src, u_all, h_src, h_ret, h_fwd, h_other, g_src, g_all,
    states_bf, grads_bf, dmat, wts, growth, shrink, attended, gained, qdec, agrad,
    kpart, vpart,
    in_sem, x_send, x_recv, a_send, a_recv,
):
    s = lax.axis_index("seq")
    y = lax.axis_index("head")
    c = s & 1
    p = s >> 1
    x = at_least(p, (NZ, 2 * NZ, 3 * NZ))
    z = p - NZ * x
    third = at_least(z, (3, 6, 9))
    z_rest = z - 3 * third
    is_owner = z_rest != 2
    zi = 2 * third + jnp.minimum(z_rest, 1)
    my_tile = x * OWN_Z + zi
    partner = (s + 1 - 2 * c, y)
    mine, theirs = 2 * c, 2 - 2 * c
    xs = {dx: (x + dx) & (NX - 1) for dx in X_STEPS}

    def load(slot, *pairs):
        for src, dst in pairs:
            pltpu.make_async_copy(src, dst, in_sem.at[slot]).start()

    def arrived(slot, dst):
        pltpu.make_async_copy(dst, dst, in_sem.at[slot]).wait()

    def load_heads(slot, src, dst):
        load(slot, *((src.at[:, pl.ds(h * DH, DH)], dst.at[h]) for h in range(HL)))

    load(0, (ld_hbm, ld))
    load_heads(1, k_hbm, k)
    load_heads(2, v_hbm, v)
    load_heads(3, q_hbm, q)
    load_heads(4, og_hbm, og)
    load(5, (gain_hbm, gain))
    load(6, (sin_hbm.at[c * TILES + my_tile], tile_in))
    load(7, (sout_hbm.at[c * TILES + my_tile], tile_out))

    def to_chips(send):
        def ring(step, steps):
            zt = z + far_first(step, NZ)
            zt = jnp.where(zt >= NZ, zt - NZ, zt)
            for dx in steps:
                send(xs[dx] * NZ + zt)

        def body(step, carry):
            ring(step, X_STEPS)
            return carry

        lax.fori_loop(0, NZ - 1, body, 0)
        ring(NZ - 1, X_STEPS[:-1])

    barrier = pltpu.get_barrier_semaphore()

    def greet(s_there, y_there):
        pl.semaphore_signal(barrier, inc=1, device_id=(s_there, y_there), device_id_type=MESH)

    to_chips(lambda chip: greet(chip * 2 + c, y))
    for dy in Y_STEPS:
        greet(s, (y + dy) & (NY - 1))
    greet(*partner)

    cum_pad[...] = jnp.zeros_like(cum_pad)
    arrived(0, ld)
    cum_pad[0:HL, :] = ld[...]
    cum = cum_pad[0:8, :]
    lane = lax.broadcasted_iota(jnp.int32, (8, TOK), 1)
    for shift in (1, 2, 4, 8, 16, 32, 64, 128):
        cum = cum + jnp.where(lane >= shift, pltpu.roll(cum, shift, 1), 0.0)
    cum_pad[0:8, :] = cum
    cum_col[...] = cum_pad[...].T
    bl = jnp.broadcast_to(cum[:, TOK - 1 : TOK], (8, DH))
    bl_mine[...] = bl

    arrived(1, k)
    arrived(2, v)
    for h in range(HL):
        fade = jnp.exp(cum_col[TOK - 1 : TOK, h : h + 1] - cum_col[:, h : h + 1])
        shrink[h] = jnp.broadcast_to(fade, (TOK, DH))
        key_decayed = (k[h].astype(F32) * shrink[h]).astype(BF16)
        summ[h] = dot(key_decayed, v[h], TN)

    pl.semaphore_wait(barrier, CHIPS - 1 + NY)

    def swap(slot, src, dst):
        copy = pltpu.make_async_remote_copy(
            src_ref=src, dst_ref=dst, send_sem=x_send.at[slot], recv_sem=x_recv.at[slot],
            device_id=partner, device_id_type=MESH,
        )
        copy.start()
        return copy

    swap_bl = swap(0, bl_mine, bl_other)
    swap_summ = swap(1, summ.at[pl.ds(theirs, 2)], summ_recv)

    def push(src, dst, slot, s_there, y_there):
        pltpu.make_async_remote_copy(
            src_ref=src, dst_ref=dst, send_sem=a_send.at[slot], recv_sem=a_recv.at[slot],
            device_id=(s_there, y_there), device_id_type=MESH,
        ).start()

    def to_owners(src_of, dst, slot, keep):
        def ring(step, steps):
            zt = (zi + far_first(step, OWN_Z)) & (OWN_Z - 1)
            z_there = (zt >> 1) * 3 + (zt & 1)
            for dx in steps:
                push(src_of(xs[dx] * OWN_Z + zt), dst.at[p], slot, (xs[dx] * NZ + z_there) * 2 + c, y)

        def body(step, carry):
            ring(step, X_STEPS)
            return carry

        lax.fori_loop(0, OWN_Z - 1, body, 0)
        ring(OWN_Z - 1, X_STEPS[:-1])

        @pl.when(jnp.logical_not(is_owner))
        def _():
            ring(OWN_Z - 1, X_STEPS[-1:])

        @pl.when(is_owner)
        def _():
            dst[p] = keep()

    def drain(sem, ref, count):
        window = ref.at[pl.ds(0, count)]
        pltpu.make_async_copy(window, window, sem).wait()

    def drain_tiles(sem, ref, count=TILES):
        @pl.when(is_owner)
        def _():
            drain(sem, ref, count - 1)

        @pl.when(jnp.logical_not(is_owner))
        def _():
            drain(sem, ref, count)

    swap_bl.wait_recv()
    e_mine = jnp.exp(bl_mine[...])
    e_other = jnp.exp(bl_other[...])
    e_chip = jnp.exp(bl_mine[...] + bl_other[...])
    for h in range(HL):
        dec_src[h] = e_chip[h : h + 1, :]
    to_owners(
        lambda tile: dec_src.at[mine + tile // 16], dec_all, 0, lambda: dec_src[mine + my_tile // 16]
    )

    first = c == 0

    def pick_rows(value):
        return [jnp.where(first, value[i : i + 1, :], value[2 + i : 3 + i, :]) for i in range(2)]

    e_first = jnp.where(first, e_mine, e_other)
    e_second = jnp.where(first, e_other, e_mine)
    e_first_rows, e_second_rows = pick_rows(e_first), pick_rows(e_second)

    swap_summ.wait_recv()
    for i in range(2):
        own, other = summ[mine + i], summ_recv[i]
        early = jnp.where(first, own, other)
        late = jnp.where(first, other, own)
        t_src[16 * i : 16 * i + 16] = (e_second_rows[i] * early + late).reshape(16, 8, DH)
    to_owners(lambda tile: t_src.at[tile], t_all, 1, lambda: t_src[my_tile])

    arrived(3, q)
    row_id = lax.broadcasted_iota(jnp.int32, (TOK, TOK), 0)
    col_id = lax.broadcasted_iota(jnp.int32, (TOK, TOK), 1)
    for h in range(HL):
        col = cum_col[:, h : h + 1]
        spread = col - cum_pad[h : h + 1, :]
        decay = jnp.where(row_id >= col_id, jnp.exp(jnp.minimum(spread, 0.0)), 0.0)
        dmat[h] = decay
        weights = (dot(q[h], k[h], NT) * decay).astype(BF16)
        wts[h] = weights
        attended[h] = dot(weights, v[h], NN)
        growth[h] = jnp.broadcast_to(jnp.exp(col), (TOK, DH))
        qdec[h] = (q[h].astype(F32) * growth[h]).astype(BF16)

    arrived(6, tile_in)
    arrived(7, tile_out)

    @pl.when(is_owner)
    def _():
        drain(a_recv.at[0], dec_all, CHIPS - 1)
        drain(a_recv.at[1], t_all, CHIPS - 1)

        def body(chip, state):
            p_src[chip] = state
            return dec_all[chip] * state + t_all[chip]

        lax.fori_loop(0, CHIPS, body, tile_in[...], unroll=4)
        to_chips(lambda chip: push(p_src.at[chip], p_ret.at[c, my_tile], 2, chip * 2 + c, y))
        p_ret[c, my_tile] = p_src[p]

    arrived(4, og)
    arrived(5, gain)
    for h in range(HL):
        gained[h] = gain[:, h * DH : (h + 1) * DH] * og[h].astype(F32)

    drain_tiles(a_recv.at[2], p_ret.at[c])
    for i in range(2):
        chip_state = p_ret[c, 16 * i : 16 * i + 16].reshape(DH, DH)
        after = e_first_rows[i] * chip_state + jnp.where(first, summ[mine + i], summ_recv[i])
        p_fwd[i] = jnp.where(first, after, chip_state)
        states_bf[mine + i] = jnp.where(first, chip_state, after).astype(BF16)
    swap_state = swap(2, p_fwd, p_other)

    def attend(h, square, inner):
        state_part = dot(q[h], states_bf[h], NN)
        out = attended[h] + growth[h] * state_part
        attended[h] = out
        return square + out * out, inner + gained[h] * out

    square = jnp.zeros((TOK, DH), F32)
    inner = jnp.zeros((TOK, DH), F32)
    for i in range(2):
        square, inner = attend(mine + i, square, inner)
    swap_state.wait_recv()
    for i in range(2):
        states_bf[theirs + i] = p_other[i].astype(BF16)
    for i in range(2):
        square, inner = attend(theirs + i, square, inner)

    sum_send[0:1, :] = jnp.sum(square.T, axis=0, keepdims=True)
    sum_send[1:2, :] = jnp.sum(inner.T, axis=0, keepdims=True)

    for dy in Y_STEPS:
        push(sum_send, sum_recv.at[y], 3, s, (y + dy) & (NY - 1))
    sum_recv[y] = sum_send[...]
    rows_pad[...] = jnp.zeros_like(rows_pad)
    drain(a_recv.at[3], sum_recv, NY - 1)
    total = sum_recv[0]
    for i in range(1, NY):
        total = total + sum_recv[i]
    features = HL * DH * NY
    inv_rms = lax.rsqrt(total[0:1, :] / features + EPSILON)
    rows_pad[0:1, :] = inv_rms
    rows_pad[1:2, :] = total[1:2, :] * (inv_rms * inv_rms * inv_rms) / features
    cols_pad[...] = rows_pad[...].T
    inv_col = cols_pad[:, 0:1]
    coef_col = cols_pad[:, 1:2]

    for h in range(HL):
        grad = (gained[h] * inv_col - attended[h] * coef_col).astype(BF16)
        agrad[h] = grad
        gsum[h] = dot(qdec[h], grad, TN)
    swap_grad = swap(3, gsum.at[pl.ds(theirs, 2)], gsum_recv)

    def score_part(h):
        score = (dot(agrad[h], v[h], NT) * dmat[h]).astype(BF16)
        query_grad = dot(score, k[h], NN) + growth[h] * dot(agrad[h], states_bf[h], NT)
        qg[h] = query_grad.astype(BF16)
        kpart[h] = dot(score, q[h], TN)
        vpart[h] = dot(wts[h], agrad[h], TN)

    swap_grad.wait_recv()
    for i in range(2):
        own, other = gsum[mine + i], gsum_recv[i]
        early = jnp.where(first, own, other)
        late = jnp.where(first, other, own)
        u_src[16 * i : 16 * i + 16] = (e_first_rows[i] * late + early).reshape(16, 8, DH)
    to_owners(lambda tile: u_src.at[tile], u_all, 4, lambda: u_src[my_tile])

    for h in range(HL):
        score_part(h)

    @pl.when(is_owner)
    def _():
        drain(a_recv.at[4], u_all, CHIPS - 1)

        def body(step, grad):
            chip = CHIPS - 1 - step
            h_src[chip] = grad
            return dec_all[chip] * grad + u_all[chip]

        g_src[...] = lax.fori_loop(0, CHIPS, body, tile_out[...], unroll=4)
        for dz in (6, 5, 7, 4, 8, 3, 9, 2, 10, 1, 11):
            zt = z + dz
            zt = jnp.where(zt >= NZ, zt - NZ, zt)
            push(g_src, g_all.at[c, my_tile], 6, (x * NZ + zt) * 2 + c, y)
        to_chips(lambda chip: push(h_src.at[chip], h_ret.at[c, my_tile], 5, chip * 2 + c, y))
        h_ret[c, my_tile] = h_src[p]
        g_all[c, my_tile] = g_src[...]

    drain_tiles(a_recv.at[6], g_all.at[c], OWN_Z)
    line = g_all.at[c, pl.ds(x * OWN_Z, OWN_Z)]
    for dx in X_STEPS[:-1]:
        push(line, line, 7, (xs[dx] * NZ + z) * 2 + c, y)

    drain_tiles(a_recv.at[5], h_ret.at[c])
    for i in range(2):
        chip_grad = h_ret[c, 16 * i : 16 * i + 16].reshape(DH, DH)
        before = e_second_rows[i] * chip_grad + jnp.where(first, gsum_recv[i], gsum[mine + i])
        h_fwd[i] = jnp.where(first, chip_grad, before)
        grads_bf[mine + i] = jnp.where(first, before, chip_grad).astype(BF16)
    swap_back = swap(4, h_fwd, h_other)

    def finish(h):
        key_grad = kpart[h] + shrink[h] * dot(v[h], grads_bf[h], NT)
        kg[h] = key_grad.astype(BF16)
        value_grad = vpart[h] + shrink[h] * dot(k[h], grads_bf[h], NN)
        vg[h] = value_grad.astype(BF16)

    for i in range(2):
        finish(mine + i)
    swap_back.wait_recv()
    for i in range(2):
        grads_bf[theirs + i] = h_other[i].astype(BF16)
    for i in range(2):
        finish(theirs + i)

    drain(a_recv.at[7], g_all.at[c], TILES - OWN_Z)
    swap_slab = swap(5, g_all.at[c], g_all.at[c])
    swap_slab.wait_recv()
    sg[...] = g_all[...]

    for copy in (swap_bl, swap_summ, swap_state, swap_grad, swap_back, swap_slab):
        copy.wait_send()
    for slot, ref in ((0, dec_all), (1, t_src), (4, u_src)):
        drain_tiles(a_send.at[slot], ref)
    drain(a_send.at[3], sum_recv, NY - 1)

    @pl.when(is_owner)
    def _():
        for slot in (2, 5):
            drain(a_send.at[slot], p_src, CHIPS - 1)
        drain(a_send.at[6], p_src, NZ - 1)

    drain(a_send.at[7], p_src, TILES - OWN_Z)


def store_kernel(qg, kg, vg, sg, qg_out, kg_out, vg_out, sg_out, sem):
    copies = [pltpu.make_async_copy(sg, sg_out, sem.at[3 * HL])]
    for index, (src, dst) in enumerate(((qg, qg_out), (kg, kg_out), (vg, vg_out))):
        for h in range(HL):
            copies.append(pltpu.make_async_copy(src.at[h], dst.at[:, pl.ds(h * DH, DH)], sem.at[index * HL + h]))
    for copy in copies:
        copy.start()
    for copy in copies:
        copy.wait()


def on_device(query_rows, key_rows, value_rows, log_decay, out_grad, norm_gain, state_in, state_out_grad):
    hbm = pl.BlockSpec(memory_space=pltpu.HBM)
    vmem = pl.BlockSpec(memory_space=pltpu.VMEM)

    def vm(*shape, dtype=F32):
        return pltpu.VMEM(shape, dtype)

    tiles = vm(TILES, 8, DH)
    landing = vm(CHIPS, 8, DH)
    halves = vm(2, TILES, 8, DH)
    pair = vm(2, DH, DH)
    heads = vm(HL, TOK, DH)
    heads_bf = vm(HL, TOK, DH, dtype=BF16)
    state = vm(HL, DH, DH)
    state_bf = vm(HL, DH, DH, dtype=BF16)
    dma = pltpu.SemaphoreType.DMA
    rows = jax.ShapeDtypeStruct(query_rows.shape, BF16)
    slab = jax.ShapeDtypeStruct((2, TILES, 8, DH), F32)
    by_head = vm(HL, TOK, DH, dtype=BF16)
    arrays = (
        query_rows, key_rows, value_rows, log_decay, out_grad, norm_gain.reshape(1, HL * DH),
        state_in.reshape(2 * TILES, 8, DH), state_out_grad.reshape(2 * TILES, 8, DH),
    )
    grads = pl.pallas_call(
        kernel,
        out_shape=(by_head, by_head, by_head, vm(2, TILES, 8, DH)),
        in_specs=[hbm] * 8,
        out_specs=(vmem,) * 4,
        scratch_shapes=[
            heads_bf, heads_bf, heads_bf, heads_bf, vm(1, HL * DH), vm(HL, TOK), vm(8, DH), vm(8, DH),
            vm(DH, TOK), vm(TOK, DH), vm(8, DH), vm(8, DH), vm(HL, 1, DH), vm(CHIPS, 1, DH),
            vm(2, TOK), vm(NY, 2, TOK), vm(DH, TOK), vm(TOK, DH),
            state, pair, tiles, landing, landing, halves, pair, pair,
            state, pair, tiles, landing, landing, halves, pair, pair, vm(8, DH), halves,
            state_bf, state_bf, vm(HL, TOK, TOK), vm(HL, TOK, TOK, dtype=BF16), heads, heads, heads, heads, heads_bf, heads_bf,
            heads, heads,
            dma((8,)), dma((6,)), dma((6,)), dma((8,)), dma((8,)),
        ],
        compiler_params=pltpu.CompilerParams(
            collective_id=0, has_side_effects=True, vmem_limit_bytes=32 * 1024 * 1024
        ),
    )(*(pltpu.with_memory_space_constraint(array, pltpu.HBM) for array in arrays))
    qg, kg, vg, sg = pl.pallas_call(
        store_kernel,
        out_shape=(rows, rows, rows, slab),
        in_specs=[vmem] * 4,
        out_specs=(hbm,) * 4,
        scratch_shapes=[dma((3 * HL + 1,))],
        compiler_params=pltpu.CompilerParams(vmem_limit_bytes=4 * 1024 * 1024),
    )(*(pltpu.with_memory_space_constraint(grad, pltpu.VMEM) for grad in grads))
    return qg, kg, vg, sg.reshape(HL, DH, DH)


def solution(mesh):
    wide = P("seq", "head")
    state = P("head", None, None)
    return jax.shard_map(
        on_device,
        mesh=mesh,
        in_specs=(wide, wide, wide, P("head", "seq"), wide, P("head"), state, state),
        out_specs=(wide, wide, wide, state),
        check_vma=False,
    )
```

time: 88.3 us -> 71.2 us (0.81)
  local copies, waits for them, and re-layouts: 9.87 us -> 0 us
  Pallas kernels: 77.4 us -> 70.4 us
    unnamed x20 -> x0, local copies, waits for them, and re-layouts: 9.87 us -> none
    pallas_call x1 -> x2, Pallas kernels: 77.4 us -> 70.4 us  [the longest x1 69.4 us: on_device(): pl.pallas_call(kernel, out_shape=(by_head, by_head, by_head, vm(2, TILES,...]
where the time goes in v2:
time: 71.2 us; the launch traced here: 71.1 us
  Pallas kernels  70.4 us (99%)
    pallas_call x1, Pallas kernels, on_device(): pl.pallas_call(kernel, out_shape=(by_head, by_head, by_head, vm(2, TILES,...  69.4 us

profile of v2, /device:TPU:1, one launch (start us, length us, event | category | flops | bytes accessed | tf_op | source)
XLA Modules:
  0.0 71.1 jit_solution(2322689063688021553)
XLA Ops:
  0.6 69.4 %shard_map.111 = (bf16[4,256,128]{2,1,0:T(8,128)(2,1)S(1)}, bf16[4,256,128]{2,1,0:T(8,128)(2,1)S(1)}, bf16[4,256,128]{2,1,0:T(8,128)(2,1)S(1)}, f32[2,32,8,128]{3,2,1,0:T(8,128)S(1)}) custom-call(bf16[256,512]{1,0:T(8,128)(2,1)} %q_hbm.1, bf16[256,512]{1,0:T(8,128)(2,1)} %k_hbm.1, bf16[256,512]{1,0:T(8,128)(2,1)} %v_hbm.1, f32[4,256]{1,0:T(4,128)} %ld_hbm.1, ...), custom_call_target="tpu_custom_call" | custom-call | tf_op jit(solution)/shard_map/pallas_call | solution.py:411
  70.0 1.1 %shard_map.112 = (bf16[256,512]{1,0:T(8,128)(2,1)}, bf16[256,512]{1,0:T(8,128)(2,1)}, bf16[256,512]{1,0:T(8,128)(2,1)}, f32[2,32,8,128]{3,2,1,0:T(8,128)}) custom-call(bf16[4,256,128]{2,1,0:T(8,128)(2,1)S(1)} %get-tuple-element.12.qg, bf16[4,256,128]{2,1,0:T(8,128)(2,1)S(1)} %get-tuple-element.13.kg, bf16[4,256,128]{2,1,0:T(8,128)(2,1)S(1)} %get-tuple-element.14.vg, ...), custom_call_target="tpu_custom_call" | custom-call | tf_op jit(solution)/shard_map/pallas_call | solution.py:430

commit v3 on v2

v3 whole, which is shorter than its diff:
```python
import jax
import jax.numpy as jnp
from jax import lax
from jax.experimental import pallas as pl
from jax.experimental.pallas import tpu as pltpu
from jax.sharding import PartitionSpec as P

EPSILON = 1e-06
MESH = pl.DeviceIdType.MESH
F32 = jnp.float32
BF16 = jnp.bfloat16

NX, NZ, NY = 4, 12, 8
CHIPS = NX * NZ
HL, TOK, DH = 4, 256, 128
TILES = 32
OWN_Z = 8
X_STEPS = (2, 1, 3, 0)
Y_STEPS = (4, 3, 5, 2, 6, 1, 7)


def far_first(step, count):
    return count // 2 + ((step + 1) >> 1) * (1 - 2 * (step & 1))


def dot(a, b, dims):
    return lax.dot_general(a, b, (dims, ((), ())), preferred_element_type=F32)


NN = ((1,), (0,))
NT = ((1,), (1,))
TN = ((0,), (0,))


def at_least(value, bounds):
    return sum((value >= bound).astype(jnp.int32) for bound in bounds)


def kernel(
    q_hbm, k_hbm, v_hbm, ld_hbm, og_hbm, gain_hbm, sin_hbm, sout_hbm,
    qg, kg, vg, sg,
    q, k, v, og, gain, ld, tile_in, tile_out,
    cum_pad, cum_col, cum_recv, cum_two, cum_two_col, dec_src, dec_all,
    sum_send, sum_recv, rows_pad, cols_pad,
    summ, summ_recv, s_first, t_src, t_all, p_src, p_ret,
    gsum, u_src, u_all, h_src, h_ret, h_fwd, h_other, g_src, g_all,
    in_src, in_recv, q2, k2, v2, og2,
    states_bf, grads_bf, dmat, wts, growth, shrink, attended, gained, qdec, agrad,
    qpart, kpart, vpart, qpart_recv, kpart_recv, vpart_recv,
    in_sem, x_send, x_recv, a_send, a_recv,
):
    s = lax.axis_index("seq")
    y = lax.axis_index("head")
    c = s & 1
    p = s >> 1
    x = at_least(p, (NZ, 2 * NZ, 3 * NZ))
    z = p - NZ * x
    third = at_least(z, (3, 6, 9))
    z_rest = z - 3 * third
    is_owner = z_rest != 2
    zi = 2 * third + jnp.minimum(z_rest, 1)
    my_tile = x * OWN_Z + zi
    partner = (s + 1 - 2 * c, y)
    mine, theirs = 2 * c, 2 - 2 * c
    first = c == 0
    xs = {dx: (x + dx) & (NX - 1) for dx in X_STEPS}

    def load(slot, *pairs):
        for src, dst in pairs:
            pltpu.make_async_copy(src, dst, in_sem.at[slot]).start()

    def arrived(slot, dst):
        pltpu.make_async_copy(dst, dst, in_sem.at[slot]).wait()

    def load_heads(slot, src, dst):
        load(slot, *((src.at[:, pl.ds(h * DH, DH)], dst.at[h]) for h in range(HL)))

    load(0, (ld_hbm, ld))
    load_heads(1, k_hbm, k)
    load_heads(2, v_hbm, v)
    load_heads(3, q_hbm, q)
    load_heads(4, og_hbm, og)
    load(5, (gain_hbm, gain))
    load(6, (sin_hbm.at[c * TILES + my_tile], tile_in))
    load(7, (sout_hbm.at[c * TILES + my_tile], tile_out))

    def to_chips(send):
        def ring(step, steps):
            zt = z + far_first(step, NZ)
            zt = jnp.where(zt >= NZ, zt - NZ, zt)
            for dx in steps:
                send(xs[dx] * NZ + zt)

        def body(step, carry):
            ring(step, X_STEPS)
            return carry

        lax.fori_loop(0, NZ - 1, body, 0)
        ring(NZ - 1, X_STEPS[:-1])

    barrier = pltpu.get_barrier_semaphore()

    def greet(s_there, y_there):
        pl.semaphore_signal(barrier, inc=1, device_id=(s_there, y_there), device_id_type=MESH)

    to_chips(lambda chip: greet(chip * 2 + c, y))
    for dy in Y_STEPS:
        for core in range(2):
            greet(2 * p + core, (y + dy) & (NY - 1))
    greet(*partner)

    cum_pad[...] = jnp.zeros_like(cum_pad)
    arrived(0, ld)
    cum_pad[0:HL, :] = ld[...]
    cum = cum_pad[0:8, :]
    lane = lax.broadcasted_iota(jnp.int32, (8, TOK), 1)
    for shift in (1, 2, 4, 8, 16, 32, 64, 128):
        cum = cum + jnp.where(lane >= shift, pltpu.roll(cum, shift, 1), 0.0)
    cum_pad[0:8, :] = cum
    cum_col[...] = cum_pad[...].T

    arrived(1, k)
    arrived(2, v)
    for h in range(HL):
        fade = jnp.exp(cum_col[TOK - 1 : TOK, h : h + 1] - cum_col[:, h : h + 1])
        shrink[h] = jnp.broadcast_to(fade, (TOK, DH))
        key_decayed = (k[h].astype(F32) * shrink[h]).astype(BF16)
        summ[h] = dot(key_decayed, v[h], TN)

    pl.semaphore_wait(barrier, CHIPS - 1 + 2 * NY - 1)

    def swap(slot, src, dst):
        copy = pltpu.make_async_remote_copy(
            src_ref=src, dst_ref=dst, send_sem=x_send.at[slot], recv_sem=x_recv.at[slot],
            device_id=partner, device_id_type=MESH,
        )
        copy.start()
        return copy

    swap_cum = swap(0, cum_pad.at[pl.ds(0, 8)], cum_recv)
    swap_summ = swap(1, summ.at[pl.ds(theirs, 2)], summ_recv)

    def push(src, dst, slot, s_there, y_there):
        pltpu.make_async_remote_copy(
            src_ref=src, dst_ref=dst, send_sem=a_send.at[slot], recv_sem=a_recv.at[slot],
            device_id=(s_there, y_there), device_id_type=MESH,
        ).start()

    def to_owners(src_of, dst, slot, keep):
        def ring(step, steps):
            zt = (zi + far_first(step, OWN_Z)) & (OWN_Z - 1)
            z_there = (zt >> 1) * 3 + (zt & 1)
            for dx in steps:
                push(src_of(xs[dx] * OWN_Z + zt), dst.at[p], slot, (xs[dx] * NZ + z_there) * 2 + c, y)

        def body(step, carry):
            ring(step, X_STEPS)
            return carry

        lax.fori_loop(0, OWN_Z - 1, body, 0)
        ring(OWN_Z - 1, X_STEPS[:-1])

        @pl.when(jnp.logical_not(is_owner))
        def _():
            ring(OWN_Z - 1, X_STEPS[-1:])

        @pl.when(is_owner)
        def _():
            dst[p] = keep()

    def drain(sem, ref, count):
        window = ref.at[pl.ds(0, count)]
        pltpu.make_async_copy(window, window, sem).wait()

    def drain_tiles(sem, ref, count=TILES):
        @pl.when(is_owner)
        def _():
            drain(sem, ref, count - 1)

        @pl.when(jnp.logical_not(is_owner))
        def _():
            drain(sem, ref, count)

    cum_two[...] = jnp.zeros_like(cum_two)
    swap_cum.wait_recv()
    for i in range(2):
        own, other = cum_pad[pl.ds(mine + i, 1), :], cum_recv[pl.ds(mine + i, 1), :]
        cum_two[i : i + 1, :] = jnp.where(first, own, other)
        cum_two[2 + i : 3 + i, :] = jnp.where(first, other, own)
    logs = jnp.broadcast_to(cum_two[0:8, TOK - 1 : TOK], (8, DH))
    decays = jnp.exp(logs)
    first_decay = [decays[i : i + 1, :] for i in range(2)]
    second_decay = [decays[2 + i : 3 + i, :] for i in range(2)]
    for i in range(2):
        dec_src[i] = jnp.exp(logs[i : i + 1, :] + logs[2 + i : 3 + i, :])
    to_owners(lambda tile: dec_src.at[tile >> 4], dec_all, 0, lambda: dec_src[my_tile >> 4])

    swap_summ.wait_recv()
    for i in range(2):
        own, other = summ[mine + i], summ_recv[i]
        early = jnp.where(first, own, other)
        late = jnp.where(first, other, own)
        s_first[i] = early
        t_src[16 * i : 16 * i + 16] = (second_decay[i] * early + late).reshape(16, 8, DH)
    to_owners(lambda tile: t_src.at[tile], t_all, 1, lambda: t_src[my_tile])

    arrived(3, q)
    arrived(4, og)
    for n, rows in enumerate((q, k, v, og)):
        for i in range(2):
            in_src[n, i] = rows[theirs + i].astype(F32)
    swap_in = swap(2, in_src, in_recv)
    for rows, both in ((q, q2), (k, k2), (v, v2), (og, og2)):
        for i in range(2):
            both[mine + i] = rows[mine + i]
    cum_two_col[...] = cum_two[...].T
    arrived(5, gain)
    swap_in.wait_recv()
    for n, both in enumerate((q2, k2, v2, og2)):
        for i in range(2):
            both[theirs + i] = in_recv[n, i].astype(BF16)

    row_id = lax.broadcasted_iota(jnp.int32, (TOK, TOK), 0)
    col_id = lax.broadcasted_iota(jnp.int32, (TOK, TOK), 1)
    for j in range(4):
        col = cum_two_col[:, j : j + 1]
        spread = col - cum_two[j : j + 1, :]
        decay = jnp.where(row_id >= col_id, jnp.exp(jnp.minimum(spread, 0.0)), 0.0)
        dmat[j] = decay
        weights = (dot(q2[j], k2[j], NT) * decay).astype(BF16)
        wts[j] = weights
        attended[j] = dot(weights, v2[j], NN)
        growth[j] = jnp.broadcast_to(jnp.exp(col), (TOK, DH))
        qdec[j] = (q2[j].astype(F32) * growth[j]).astype(BF16)

    arrived(6, tile_in)
    arrived(7, tile_out)

    @pl.when(is_owner)
    def _():
        drain(a_recv.at[0], dec_all, CHIPS - 1)
        drain(a_recv.at[1], t_all, CHIPS - 1)

        def body(chip, state):
            p_src[chip] = state
            return dec_all[chip] * state + t_all[chip]

        lax.fori_loop(0, CHIPS, body, tile_in[...], unroll=4)
        to_chips(lambda chip: push(p_src.at[chip], p_ret.at[my_tile], 2, chip * 2 + c, y))
        p_ret[my_tile] = p_src[p]

    for j in range(4):
        gained[j] = gain[mine + j % 2] * og2[j].astype(F32)
    rows_pad[...] = jnp.zeros_like(rows_pad)

    drain_tiles(a_recv.at[2], p_ret)
    for i in range(2):
        chip_state = p_ret[16 * i : 16 * i + 16].reshape(DH, DH)
        states_bf[i] = chip_state.astype(BF16)
        states_bf[2 + i] = (first_decay[i] * chip_state + s_first[i]).astype(BF16)
    for block in range(2):
        square = jnp.zeros((TOK, DH), F32)
        inner = jnp.zeros((TOK, DH), F32)
        for j in (2 * block, 2 * block + 1):
            out = attended[j] + growth[j] * dot(q2[j], states_bf[j], NN)
            attended[j] = out
            square = square + out * out
            inner = inner + gained[j] * out
        sum_send[2 * block : 2 * block + 1, :] = jnp.sum(square.T, axis=0, keepdims=True)
        sum_send[2 * block + 1 : 2 * block + 2, :] = jnp.sum(inner.T, axis=0, keepdims=True)

    place = 2 * y + c
    for dy in Y_STEPS:
        for core in range(2):
            push(sum_send, sum_recv.at[place], 3, 2 * p + core, (y + dy) & (NY - 1))
    push(sum_send, sum_recv.at[place], 3, *partner)
    sum_recv[place] = sum_send[...]
    drain(a_recv.at[3], sum_recv, 2 * NY - 1)
    total = sum_recv[0]
    for i in range(1, 2 * NY):
        total = total + sum_recv[i]
    features = HL * DH * NY
    for block in range(2):
        inv_rms = lax.rsqrt(total[2 * block : 2 * block + 1, :] / features + EPSILON)
        coefficient = total[2 * block + 1 : 2 * block + 2, :] * (inv_rms * inv_rms * inv_rms) / features
        rows_pad[2 * block : 2 * block + 1, :] = inv_rms
        rows_pad[2 * block + 1 : 2 * block + 2, :] = coefficient
    cols_pad[...] = rows_pad[...].T

    for j in range(4):
        b = j // 2
        inv_col, coef_col = cols_pad[:, 2 * b : 2 * b + 1], cols_pad[:, 2 * b + 1 : 2 * b + 2]
        grad = (gained[j] * inv_col - attended[j] * coef_col).astype(BF16)
        agrad[j] = grad
        gsum[j] = dot(qdec[j], grad, TN)

    for i in range(2):
        u_src[16 * i : 16 * i + 16] = (first_decay[i] * gsum[2 + i] + gsum[i]).reshape(16, 8, DH)
    to_owners(lambda tile: u_src.at[tile], u_all, 4, lambda: u_src[my_tile])

    for j in range(4):
        score = (dot(agrad[j], v2[j], NT) * dmat[j]).astype(BF16)
        qpart[j] = dot(score, k2[j], NN) + growth[j] * dot(agrad[j], states_bf[j], NT)
        kpart[j] = dot(score, q2[j], TN)
        vpart[j] = dot(wts[j], agrad[j], TN)
    swap_parts = [
        swap(3 + n, part.at[pl.ds(theirs, 2)], dst)
        for n, (part, dst) in enumerate(((qpart, qpart_recv), (kpart, kpart_recv), (vpart, vpart_recv)))
    ]
    for i in range(2):
        qg[mine + i] = qpart[mine + i].astype(BF16)

    @pl.when(is_owner)
    def _():
        drain(a_recv.at[4], u_all, CHIPS - 1)

        def body(step, grad):
            chip = CHIPS - 1 - step
            h_src[chip] = grad
            return dec_all[chip] * grad + u_all[chip]

        g_src[...] = lax.fori_loop(0, CHIPS, body, tile_out[...], unroll=4)
        for dz in (6, 5, 7, 4, 8, 3, 9, 2, 10, 1, 11):
            zt = z + dz
            zt = jnp.where(zt >= NZ, zt - NZ, zt)
            push(g_src, g_all.at[c, my_tile], 6, (x * NZ + zt) * 2 + c, y)
        to_chips(lambda chip: push(h_src.at[chip], h_ret.at[my_tile], 5, chip * 2 + c, y))
        h_ret[my_tile] = h_src[p]
        g_all[c, my_tile] = g_src[...]

    for copy in swap_parts:
        copy.wait_recv()
    for i in range(2):
        qg[theirs + i] = qpart_recv[i].astype(BF16)

    drain_tiles(a_recv.at[6], g_all.at[c], OWN_Z)
    line = g_all.at[c, pl.ds(x * OWN_Z, OWN_Z)]
    for dx in X_STEPS[:-1]:
        push(line, line, 7, (xs[dx] * NZ + z) * 2 + c, y)

    drain_tiles(a_recv.at[5], h_ret)
    for i in range(2):
        after_second = h_ret[16 * i : 16 * i + 16].reshape(DH, DH)
        after_first = second_decay[i] * after_second + gsum[2 + i]
        h_fwd[i] = jnp.where(first, after_second, after_first)
        grads_bf[mine + i] = jnp.where(first, after_first, after_second).astype(BF16)
    swap_back = swap(6, h_fwd, h_other)

    def finish(h, key_part, value_part):
        kg[h] = (key_part + shrink[h] * dot(v[h], grads_bf[h], NT)).astype(BF16)
        vg[h] = (value_part + shrink[h] * dot(k[h], grads_bf[h], NN)).astype(BF16)

    for i in range(2):
        finish(mine + i, kpart[mine + i], vpart[mine + i])
    swap_back.wait_recv()
    for i in range(2):
        grads_bf[theirs + i] = h_other[i].astype(BF16)
    for i in range(2):
        finish(theirs + i, kpart_recv[i], vpart_recv[i])

    drain(a_recv.at[7], g_all.at[c], TILES - OWN_Z)
    swap_slab = swap(7, g_all.at[c], g_all.at[c])
    swap_slab.wait_recv()
    sg[...] = g_all[...]

    for copy in (swap_cum, swap_summ, swap_in, *swap_parts, swap_back, swap_slab):
        copy.wait_send()
    for slot, ref in ((0, dec_all), (1, t_src), (4, u_src)):
        drain_tiles(a_send.at[slot], ref)
    drain(a_send.at[3], sum_recv, 2 * NY - 1)

    @pl.when(is_owner)
    def _():
        for slot in (2, 5):
            drain(a_send.at[slot], p_src, CHIPS - 1)
        drain(a_send.at[6], p_src, NZ - 1)

    drain(a_send.at[7], p_src, TILES - OWN_Z)


def store_kernel(qg, kg, vg, sg, qg_out, kg_out, vg_out, sg_out, sem):
    copies = [pltpu.make_async_copy(sg, sg_out, sem.at[3 * HL])]
    for index, (src, dst) in enumerate(((qg, qg_out), (kg, kg_out), (vg, vg_out))):
        for h in range(HL):
            copies.append(pltpu.make_async_copy(src.at[h], dst.at[:, pl.ds(h * DH, DH)], sem.at[index * HL + h]))
    for copy in copies:
        copy.start()
    for copy in copies:
        copy.wait()


def on_device(query_rows, key_rows, value_rows, log_decay, out_grad, norm_gain, state_in, state_out_grad):
    hbm = pl.BlockSpec(memory_space=pltpu.HBM)
    vmem = pl.BlockSpec(memory_space=pltpu.VMEM)

    def vm(*shape, dtype=F32):
        return pltpu.VMEM(shape, dtype)

    tiles = vm(TILES, 8, DH)
    landing = vm(CHIPS, 8, DH)
    pair = vm(2, DH, DH)
    heads = vm(HL, TOK, DH)
    block_pair = vm(2, TOK, DH)
    heads_bf = vm(HL, TOK, DH, dtype=BF16)
    state = vm(HL, DH, DH)
    state_bf = vm(HL, DH, DH, dtype=BF16)
    dma = pltpu.SemaphoreType.DMA
    rows = jax.ShapeDtypeStruct(query_rows.shape, BF16)
    slab = jax.ShapeDtypeStruct((2, TILES, 8, DH), F32)
    by_head = vm(HL, TOK, DH, dtype=BF16)
    arrays = (
        query_rows, key_rows, value_rows, log_decay, out_grad, norm_gain.reshape(HL, 1, DH),
        state_in.reshape(2 * TILES, 8, DH), state_out_grad.reshape(2 * TILES, 8, DH),
    )
    grads = pl.pallas_call(
        kernel,
        out_shape=(by_head, by_head, by_head, vm(2, TILES, 8, DH)),
        in_specs=[hbm] * 8,
        out_specs=(vmem,) * 4,
        scratch_shapes=[
            heads_bf, heads_bf, heads_bf, heads_bf, vm(HL, 1, DH), vm(HL, TOK), vm(8, DH), vm(8, DH),
            vm(DH, TOK), vm(TOK, DH), vm(8, TOK), vm(DH, TOK), vm(TOK, DH), vm(2, 1, DH), vm(CHIPS, 1, DH),
            vm(4, TOK), vm(2 * NY, 4, TOK), vm(DH, TOK), vm(TOK, DH),
            state, pair, pair, tiles, landing, landing, tiles,
            state, tiles, landing, landing, tiles, pair, pair, vm(8, DH), vm(2, TILES, 8, DH),
            vm(4, 2, TOK, DH), vm(4, 2, TOK, DH), heads_bf, heads_bf, heads_bf, heads_bf,
            state_bf, state_bf, vm(HL, TOK, TOK), vm(HL, TOK, TOK, dtype=BF16), heads, heads, heads, heads, heads_bf, heads_bf,
            heads, heads, heads, block_pair, block_pair, block_pair,
            dma((8,)), dma((8,)), dma((8,)), dma((8,)), dma((8,)),
        ],
        compiler_params=pltpu.CompilerParams(
            collective_id=0, has_side_effects=True, vmem_limit_bytes=32 * 1024 * 1024
        ),
    )(*(pltpu.with_memory_space_constraint(array, pltpu.HBM) for array in arrays))
    qg, kg, vg, sg = pl.pallas_call(
        store_kernel,
        out_shape=(rows, rows, rows, slab),
        in_specs=[vmem] * 4,
        out_specs=(hbm,) * 4,
        scratch_shapes=[dma((3 * HL + 1,))],
        compiler_params=pltpu.CompilerParams(vmem_limit_bytes=4 * 1024 * 1024),
    )(*(pltpu.with_memory_space_constraint(grad, pltpu.VMEM) for grad in grads))
    return qg, kg, vg, sg.reshape(HL, DH, DH)


def solution(mesh):
    wide = P("seq", "head")
    state = P("head", None, None)
    return jax.shard_map(
        on_device,
        mesh=mesh,
        in_specs=(wide, wide, wide, P("head", "seq"), wide, P("head"), state, state),
        out_specs=(wide, wide, wide, state),
        check_vma=False,
    )
```

time: 71.2 us -> 69.5 us (0.976)
  Pallas kernels: 70.4 us -> 68.7 us
    pallas_call x1, Pallas kernels: 69.4 us -> 67.6 us  [on_device(): pl.pallas_call(kernel, out_shape=(by_head, by_head, by_head, vm(2, TILES,...]
where the time goes in v3:
time: 69.5 us; the launch traced here: 69.3 us
  Pallas kernels  68.7 us (99%)
    pallas_call x1, Pallas kernels, on_device(): pl.pallas_call(kernel, out_shape=(by_head, by_head, by_head, vm(2, TILES,...  67.6 us

profile of v3, /device:TPU:1, one launch (start us, length us, event | category | flops | bytes accessed | tf_op | source)
XLA Modules:
  0.0 69.3 jit_solution(9162002226218555230)
XLA Ops:
  0.6 67.6 %shard_map.111 = (bf16[4,256,128]{2,1,0:T(8,128)(2,1)S(1)}, bf16[4,256,128]{2,1,0:T(8,128)(2,1)S(1)}, bf16[4,256,128]{2,1,0:T(8,128)(2,1)S(1)}, f32[2,32,8,128]{3,2,1,0:T(8,128)S(1)}) custom-call(bf16[256,512]{1,0:T(8,128)(2,1)} %q_hbm.1, bf16[256,512]{1,0:T(8,128)(2,1)} %k_hbm.1, bf16[256,512]{1,0:T(8,128)(2,1)} %v_hbm.1, f32[4,256]{1,0:T(4,128)} %ld_hbm.1, ...), custom_call_target="tpu_custom_call" | custom-call | tf_op jit(solution)/shard_map/pallas_call | solution.py:415
  68.3 1.1 %shard_map.112 = (bf16[256,512]{1,0:T(8,128)(2,1)}, bf16[256,512]{1,0:T(8,128)(2,1)}, bf16[256,512]{1,0:T(8,128)(2,1)}, f32[2,32,8,128]{3,2,1,0:T(8,128)}) custom-call(bf16[4,256,128]{2,1,0:T(8,128)(2,1)S(1)} %get-tuple-element.12.qg, bf16[4,256,128]{2,1,0:T(8,128)(2,1)S(1)} %get-tuple-element.13.kg, bf16[4,256,128]{2,1,0:T(8,128)(2,1)S(1)} %get-tuple-element.14.vg, ...), custom_call_target="tpu_custom_call" | custom-call | tf_op jit(solution)/shard_map/pallas_call | solution.py:435

commit v4 on v3

--- a/solution.py
+++ b/solution.py
@@ -45,7 +45,7 @@
     summ, summ_recv, s_first, t_src, t_all, p_src, p_ret,
     gsum, u_src, u_all, h_src, h_ret, h_fwd, h_other, g_src, g_all,
     in_src, in_recv, q2, k2, v2, og2,
-    states_bf, grads_bf, dmat, wts, growth, shrink, attended, gained, qdec, agrad,
+    states_bf, grads_bf, dmat, wts, growth, shrink, attended, gained, qdec_t, agrad,
     qpart, kpart, vpart, qpart_recv, kpart_recv, vpart_recv,
     in_sem, x_send, x_recv, a_send, a_recv,
 ):
@@ -231,7 +231,7 @@
         wts[j] = weights
         attended[j] = dot(weights, v2[j], NN)
         growth[j] = jnp.broadcast_to(jnp.exp(col), (TOK, DH))
-        qdec[j] = (q2[j].astype(F32) * growth[j]).astype(BF16)
+        qdec_t[j] = (q2[j].astype(F32) * growth[j]).T.astype(BF16)
 
     arrived(6, tile_in)
     arrived(7, tile_out)
@@ -287,12 +287,13 @@
         rows_pad[2 * block + 1 : 2 * block + 2, :] = coefficient
     cols_pad[...] = rows_pad[...].T
 
-    for j in range(4):
-        b = j // 2
-        inv_col, coef_col = cols_pad[:, 2 * b : 2 * b + 1], cols_pad[:, 2 * b + 1 : 2 * b + 2]
-        grad = (gained[j] * inv_col - attended[j] * coef_col).astype(BF16)
-        agrad[j] = grad
-        gsum[j] = dot(qdec[j], grad, TN)
+    for block in range(2):
+        inv_wide = jnp.broadcast_to(cols_pad[:, 2 * block : 2 * block + 1], (TOK, DH))
+        coef_wide = jnp.broadcast_to(cols_pad[:, 2 * block + 1 : 2 * block + 2], (TOK, DH))
+        for j in (2 * block, 2 * block + 1):
+            grad = (gained[j] * inv_wide - attended[j] * coef_wide).astype(BF16)
+            agrad[j] = grad
+            gsum[j] = dot(qdec_t[j], grad, NN)
 
     for i in range(2):
         u_src[16 * i : 16 * i + 16] = (first_decay[i] * gsum[2 + i] + gsum[i]).reshape(16, 8, DH)
@@ -336,7 +337,8 @@
     drain_tiles(a_recv.at[6], g_all.at[c], OWN_Z)
     line = g_all.at[c, pl.ds(x * OWN_Z, OWN_Z)]
     for dx in X_STEPS[:-1]:
-        push(line, line, 7, (xs[dx] * NZ + z) * 2 + c, y)
+        push(line, line, 6 + dx, (xs[dx] * NZ + z) * 2 + c, y)
+    swap_lines = [swap(7, line, line)]
 
     drain_tiles(a_recv.at[5], h_ret)
     for i in range(2):
@@ -358,12 +360,15 @@
     for i in range(2):
         finish(theirs + i, kpart_recv[i], vpart_recv[i])
 
-    drain(a_recv.at[7], g_all.at[c], TILES - OWN_Z)
-    swap_slab = swap(7, g_all.at[c], g_all.at[c])
-    swap_slab.wait_recv()
+    for dx in (1, 3, 2):
+        drain(a_recv.at[6 + dx], g_all.at[c], OWN_Z)
+        line = g_all.at[c, pl.ds(((x - dx) & (NX - 1)) * OWN_Z, OWN_Z)]
+        swap_lines.append(swap(7 + dx, line, line))
+    for copy in swap_lines:
+        copy.wait_recv()
     sg[...] = g_all[...]
 
-    for copy in (swap_cum, swap_summ, swap_in, *swap_parts, swap_back, swap_slab):
+    for copy in (swap_cum, swap_summ, swap_in, *swap_parts, swap_back, *swap_lines):
         copy.wait_send()
     for slot, ref in ((0, dec_all), (1, t_src), (4, u_src)):
         drain_tiles(a_send.at[slot], ref)
@@ -375,7 +380,8 @@
             drain(a_send.at[slot], p_src, CHIPS - 1)
         drain(a_send.at[6], p_src, NZ - 1)
 
-    drain(a_send.at[7], p_src, TILES - OWN_Z)
+    for dx in (1, 3, 2):
+        drain(a_send.at[6 + dx], p_src, OWN_Z)
 
 
 def store_kernel(qg, kg, vg, sg, qg_out, kg_out, vg_out, sg_out, sem):
@@ -424,9 +430,9 @@
             state, pair, pair, tiles, landing, landing, tiles,
             state, tiles, landing, landing, tiles, pair, pair, vm(8, DH), vm(2, TILES, 8, DH),
             vm(4, 2, TOK, DH), vm(4, 2, TOK, DH), heads_bf, heads_bf, heads_bf, heads_bf,
-            state_bf, state_bf, vm(HL, TOK, TOK), vm(HL, TOK, TOK, dtype=BF16), heads, heads, heads, heads, heads_bf, heads_bf,
+            state_bf, state_bf, vm(HL, TOK, TOK), vm(HL, TOK, TOK, dtype=BF16), heads, heads, heads, heads, vm(HL, DH, TOK, dtype=BF16), heads_bf,
             heads, heads, heads, block_pair, block_pair, block_pair,
-            dma((8,)), dma((8,)), dma((8,)), dma((8,)), dma((8,)),
+            dma((8,)), dma((11,)), dma((11,)), dma((10,)), dma((10,)),
         ],
         compiler_params=pltpu.CompilerParams(
             collective_id=0, has_side_effects=True, vmem_limit_bytes=32 * 1024 * 1024

time: 69.5 us -> 69.4 us (level)
  no operation moved by 1% of the time
where the time goes in v4:
time: 69.4 us; the launch traced here: 69.3 us
  Pallas kernels  68.6 us (99%)
    pallas_call x1, Pallas kernels, on_device(): pl.pallas_call(kernel, out_shape=(by_head, by_head, by_head, vm(2, TILES,...  67.6 us

profile of v4, /device:TPU:1, one launch (start us, length us, event | category | flops | bytes accessed | tf_op | source)
XLA Modules:
  0.0 69.3 jit_solution(15353184167687059649)
XLA Ops:
  0.6 67.6 %shard_map.111 = (bf16[4,256,128]{2,1,0:T(8,128)(2,1)S(1)}, bf16[4,256,128]{2,1,0:T(8,128)(2,1)S(1)}, bf16[4,256,128]{2,1,0:T(8,128)(2,1)S(1)}, f32[2,32,8,128]{3,2,1,0:T(8,128)S(1)}) custom-call(bf16[256,512]{1,0:T(8,128)(2,1)} %q_hbm.1, bf16[256,512]{1,0:T(8,128)(2,1)} %k_hbm.1, bf16[256,512]{1,0:T(8,128)(2,1)} %v_hbm.1, f32[4,256]{1,0:T(4,128)} %ld_hbm.1, ...), custom_call_target="tpu_custom_call" | custom-call | tf_op jit(solution)/shard_map/pallas_call | solution.py:421
  68.2 1.1 %shard_map.112 = (bf16[256,512]{1,0:T(8,128)(2,1)}, bf16[256,512]{1,0:T(8,128)(2,1)}, bf16[256,512]{1,0:T(8,128)(2,1)}, f32[2,32,8,128]{3,2,1,0:T(8,128)}) custom-call(bf16[4,256,128]{2,1,0:T(8,128)(2,1)S(1)} %get-tuple-element.12.qg, bf16[4,256,128]{2,1,0:T(8,128)(2,1)S(1)} %get-tuple-element.13.kg, bf16[4,256,128]{2,1,0:T(8,128)(2,1)S(1)} %get-tuple-element.14.vg, ...), custom_call_target="tpu_custom_call" | custom-call | tf_op jit(solution)/shard_map/pallas_call | solution.py:441

commit v5 on v4

--- a/solution.py
+++ b/solution.py
@@ -204,6 +204,22 @@
         t_src[16 * i : 16 * i + 16] = (second_decay[i] * early + late).reshape(16, 8, DH)
     to_owners(lambda tile: t_src.at[tile], t_all, 1, lambda: t_src[my_tile])
 
+    arrived(6, tile_in)
+    arrived(7, tile_out)
+
+    @pl.when(is_owner)
+    def _():
+        drain(a_recv.at[0], dec_all, CHIPS - 1)
+        drain(a_recv.at[1], t_all, CHIPS - 1)
+
+        def body(chip, state):
+            p_src[chip] = state
+            return dec_all[chip] * state + t_all[chip]
+
+        lax.fori_loop(0, CHIPS, body, tile_in[...], unroll=4)
+        to_chips(lambda chip: push(p_src.at[chip], p_ret.at[my_tile], 2, chip * 2 + c, y))
+        p_ret[my_tile] = p_src[p]
+
     arrived(3, q)
     arrived(4, og)
     for n, rows in enumerate((q, k, v, og)):
@@ -232,22 +248,6 @@
         attended[j] = dot(weights, v2[j], NN)
         growth[j] = jnp.broadcast_to(jnp.exp(col), (TOK, DH))
         qdec_t[j] = (q2[j].astype(F32) * growth[j]).T.astype(BF16)
-
-    arrived(6, tile_in)
-    arrived(7, tile_out)
-
-    @pl.when(is_owner)
-    def _():
-        drain(a_recv.at[0], dec_all, CHIPS - 1)
-        drain(a_recv.at[1], t_all, CHIPS - 1)
-
-        def body(chip, state):
-            p_src[chip] = state
-            return dec_all[chip] * state + t_all[chip]
-
-        lax.fori_loop(0, CHIPS, body, tile_in[...], unroll=4)
-        to_chips(lambda chip: push(p_src.at[chip], p_ret.at[my_tile], 2, chip * 2 + c, y))
-        p_ret[my_tile] = p_src[p]
 
     for j in range(4):
         gained[j] = gain[mine + j % 2] * og2[j].astype(F32)

time: 69.4 us -> 69.4 us (level)
  no operation moved by 1% of the time
where the time goes in v5:
time: 69.4 us; the launch traced here: 69.3 us
  Pallas kernels  68.6 us (99%)
    pallas_call x1, Pallas kernels, on_device(): pl.pallas_call(kernel, out_shape=(by_head, by_head, by_head, vm(2, TILES,...  67.6 us

profile of v5, /device:TPU:1, one launch (start us, length us, event | category | flops | bytes accessed | tf_op | source)
XLA Modules:
  0.0 69.3 jit_solution(9120385751844194574)
XLA Ops:
  0.6 67.6 %shard_map.111 = (bf16[4,256,128]{2,1,0:T(8,128)(2,1)S(1)}, bf16[4,256,128]{2,1,0:T(8,128)(2,1)S(1)}, bf16[4,256,128]{2,1,0:T(8,128)(2,1)S(1)}, f32[2,32,8,128]{3,2,1,0:T(8,128)S(1)}) custom-call(bf16[256,512]{1,0:T(8,128)(2,1)} %q_hbm.1, bf16[256,512]{1,0:T(8,128)(2,1)} %k_hbm.1, bf16[256,512]{1,0:T(8,128)(2,1)} %v_hbm.1, f32[4,256]{1,0:T(4,128)} %ld_hbm.1, ...), custom_call_target="tpu_custom_call" | custom-call | tf_op jit(solution)/shard_map/pallas_call | solution.py:421
  68.2 1.1 %shard_map.112 = (bf16[256,512]{1,0:T(8,128)(2,1)}, bf16[256,512]{1,0:T(8,128)(2,1)}, bf16[256,512]{1,0:T(8,128)(2,1)}, f32[2,32,8,128]{3,2,1,0:T(8,128)}) custom-call(bf16[4,256,128]{2,1,0:T(8,128)(2,1)S(1)} %get-tuple-element.12.qg, bf16[4,256,128]{2,1,0:T(8,128)(2,1)S(1)} %get-tuple-element.13.kg, bf16[4,256,128]{2,1,0:T(8,128)(2,1)S(1)} %get-tuple-element.14.vg, ...), custom_call_target="tpu_custom_call" | custom-call | tf_op jit(solution)/shard_map/pallas_call | solution.py:441
